TPU v7x, 32 devices: a whole 2x2x4 slice. The times are simulated.
32 devices in a mesh: tgt: 8 (over z, y), src: 4 (over x, core).
Axes of the slice: x: 2, y: 2, z: 4, core: 2. Of those that a mesh axis runs over, the one named last changes fastest.
Arguments:
- coefficients: bfloat16 [32, 4, 512, 512], P('tgt', 'src'), may hold values from -1.5 to 1.5
- factors: bfloat16 [3, 32, 4, 512, 512], P(None, 'tgt', 'src'), may hold values from -0.25 to 0.25
Outputs:
- potentials: float32 [32, 2, 256, 512], P('tgt', None, 'src')
All inputs are finite; a program needn't handle non-finite values.
Results may differ from a plain program's by a relative error of at most 0.013.
Values may be sent and summed in bfloat16 or wider, within the bound.
A program may use at most 64 MiB of HBM per device.

v0:
```python
import jax
import jax.numpy as jnp
from jax import lax
from jax.sharding import PartitionSpec as P


def partner(shard, axis, bit):
    return lax.ppermute(shard, axis, [(i, i ^ 1 << bit) for i in range(lax.axis_size(axis))])


def blend(weights, current):
    return jnp.einsum("bij,bjn->bin", weights, current, preferred_element_type=jnp.float32).astype(
        jnp.bfloat16
    )


def local(coefficients, factors):
    half_rows = coefficients.shape[2] // 2
    columns = coefficients.shape[3]
    blocks = coefficients.shape[0]
    level_count = factors.shape[0]
    bit_count = lax.axis_size("tgt").bit_length() - 1
    current = coefficients[:, 0]
    plain_levels = level_count - 1
    for section_index in range(plain_levels):
        blended = blend(factors[section_index, :, 0], current)
        received = partner(blended[:, half_rows:], "tgt", section_index % bit_count)
        current = jnp.concatenate([blended[:, :half_rows], received], axis=1)
    blended = blend(factors[level_count - 1, :, 0], current)
    terms = blended.astype(jnp.float32).reshape(blocks, 2, half_rows, columns)
    reduced = lax.psum_scatter(
        terms.astype(jnp.bfloat16), "src", scatter_dimension=2, tiled=True
    ).astype(jnp.float32)
    arrived = partner(reduced[:, 1], "tgt", (level_count - 1) % bit_count)
    result = jnp.stack([reduced[:, 0], arrived], axis=1)
    return result


def solution(mesh):
    placed = (P("tgt", "src", None, None), P(None, "tgt", "src", None, None))
    return jax.shard_map(
        local, mesh=mesh, in_specs=placed, out_specs=P("tgt", None, "src", None), check_vma=False
    )
```

profile of v0, /device:TPU:0, one launch (start us, length us, event | category | flops | bytes accessed | tf_op | source)
XLA Modules:
  0.0 133.4 jit_solution(16509707927514095550)
XLA Ops:
  6.5 0.0 copy-start
  6.5 0.0 reduce-scatter.2.cloned.1.call-start
  6.5 1.6 %copy-done = bf16[4,1,512,512]{3,2,1,0:T(8,128)(2,1)S(1)} copy-done((bf16[4,1,512,512]{3,2,1,0:T(8,128)(2,1)S(1)}, bf16[4,1,512,512]{3,2,1,0:T(8,128)(2,1)}, u32[]{:S(2)}) %copy-start) | copy-done | bytes 2097176
  8.1 0.0 copy-start.1
  8.1 3.0 %fusion.15 = bf16[4,512,512]{2,1,0:T(8,128)(2,1)S(1)} fusion(bf16[4,1,512,512]{3,2,1,0:T(8,128)(2,1)S(1)} %copy-done, bf16[3,4,1,512,512]{4,3,1,2,0:T(8,128)(2,1)} %bitcast.35), kind=kOutput, calls=%fused_computation.15 | convolution fusion | flops 1074790400 | bytes 6291456 | tf_op jit(solution)/shard_map/bij,bjn->bin/dot_general | solution.py:12
  11.1 0.1 fusion.21
  11.3 3.1 %collective-permute-start = (bf16[4,256,512]{2,1,0:T(8,128)(2,1)S(1)}, bf16[4,256,512]{2,1,0:T(8,128)(2,1)S(1)}, u32[]{:S(2)}, u32[]{:S(2)}) collective-permute-start(bf16[4,256,512]{2,1,0:T(8,128)(2,1)S(1)} %get-tuple-element.8), channel_id=1, source_target_pairs={{0,4},{4,0},{8,12},{12,8},{16,20},{20,16},{24,28},{28,24},{1,5},{5... | collective-permute-start | bytes 3145736 | tf_op jit(solution)/shard_map/ppermute | solution.py:8
  14.3 23.2 %collective-permute-done = bf16[4,256,512]{2,1,0:T(8,128)(2,1)S(1)} collective-permute-done((bf16[4,256,512]{2,1,0:T(8,128)(2,1)S(1)}, bf16[4,256,512]{2,1,0:T(8,128)(2,1)S(1)}, u32[]{:S(2)}, u32[]{:S(2)}) %collective-permute-start) | collective-permute-done | bytes 1048608 | tf_op jit(solution)/shard_map/ppermute | solution.py:8
  37.5 0.0 copy-done.1
  37.5 1.3 convert_bitcast_fusion
  38.8 0.2 fusion.20
  39.0 1.9 %collective-permute-start.1 = (bf16[4,256,512]{2,1,0:T(8,128)(2,1)S(1)}, bf16[4,256,512]{2,1,0:T(8,128)(2,1)S(1)}, u32[]{:S(2)}, u32[]{:S(2)}) collective-permute-start(bf16[4,256,512]{2,1,0:T(8,128)(2,1)S(1)} %get-tuple-element.6), channel_id=1, source_target_pairs={{0,8},{4,12},{8,0},{12,4},{16,24},{20,28},{24,16},{28,20},{1,9},{5... | collective-permute-start | bytes 3145736 | tf_op jit(solution)/shard_map/ppermute | solution.py:8
  40.8 22.5 %collective-permute-done.1 = bf16[4,256,512]{2,1,0:T(8,128)(2,1)S(1)} collective-permute-done((bf16[4,256,512]{2,1,0:T(8,128)(2,1)S(1)}, bf16[4,256,512]{2,1,0:T(8,128)(2,1)S(1)}, u32[]{:S(2)}, u32[]{:S(2)}) %collective-permute-start.1) | collective-permute-done | bytes 1048608 | tf_op jit(solution)/shard_map/ppermute | solution.py:8
  63.3 1.3 fusion.10
  64.6 1.5 %copy.6 = bf16[4,2,256,512]{3,2,0,1:T(8,128)(2,1)} copy(bf16[4,2,256,512]{3,2,1,0:T(8,128)(2,1)S(1)} %bitcast.33) | data formatting | bytes 4194304 | tf_op jit(solution)/shard_map/convert_element_type | solution.py:32
  66.1 0.0 reduce-scatter.2.cloned.1.call-update
  66.1 32.5 %reduce-scatter.2.cloned.1.call-done = bf16[4,2,64,512]{3,2,0,1:T(8,128)(2,1)} async-done(((bf16[4,2,256,512]{3,2,0,1:T(8,128)(2,1)}), bf16[4,2,64,512]{3,2,0,1:T(8,128)(2,1)}) %reduce-scatter.2.cloned.1.call-update) | async-done | bytes 524304 | tf_op jit(solution)/shard_map/reduce_scatter | solution.py:31
  98.6 1.2 convert_element_type.29
  99.8 0.1 slice_bitcast_fusion.13
  99.9 2.5 %collective-permute-start.2 = (f32[4,64,512]{2,1,0:T(8,128)S(1)}, f32[4,64,512]{2,1,0:T(8,128)S(1)}, u32[]{:S(2)}, u32[]{:S(2)}) collective-permute-start(f32[4,64,512]{2,1,0:T(8,128)S(1)} %get-tuple-element.10), channel_id=1, source_target_pairs={{0,16},{4,20},{8,24},{12,28},{16,0},{20,4},{24,8},{28,12},{1,17},{... | collective-permute-start | bytes 1572872 | tf_op jit(solution)/shard_map/ppermute | solution.py:8
  102.3 23.2 %collective-permute-done.2 = f32[4,64,512]{2,1,0:T(8,128)S(1)} collective-permute-done((f32[4,64,512]{2,1,0:T(8,128)S(1)}, f32[4,64,512]{2,1,0:T(8,128)S(1)}, u32[]{:S(2)}, u32[]{:S(2)}) %collective-permute-start.2) | collective-permute-done | bytes 524320 | tf_op jit(solution)/shard_map/ppermute | solution.py:8
  125.5 1.0 pad_maximum_fusion
Async XLA Ops:
  6.5 1.6 %copy-start = (bf16[4,1,512,512]{3,2,1,0:T(8,128)(2,1)S(1)}, bf16[4,1,512,512]{3,2,1,0:T(8,128)(2,1)}, u32[]{:S(2)}) copy-start(bf16[4,1,512,512]{3,2,1,0:T(8,128)(2,1)} %param.2) | copy-start | bytes 6291460
  6.5 92.1 %reduce-scatter.2.cloned.1.call-start = ((), (), s32[]{:S(2)}) async-start(), calls=%async_computation.1 | async-start | bytes 2621440 | tf_op jit(solution)/shard_map/reduce_scatter | solution.py:31
  8.1 29.4 %copy-start.1 = (bf16[3,4,1,512,512]{4,3,2,1,0:T(8,128)(2,1)S(1)}, bf16[3,4,1,512,512]{4,3,2,1,0:T(8,128)(2,1)}, u32[]{:S(2)}) copy-start(bf16[3,4,1,512,512]{4,3,2,1,0:T(8,128)(2,1)} %param.3) | copy-start | bytes 18874372
  11.3 26.2 %collective-permute-start = (bf16[4,256,512]{2,1,0:T(8,128)(2,1)S(1)}, bf16[4,256,512]{2,1,0:T(8,128)(2,1)S(1)}, u32[]{:S(2)}, u32[]{:S(2)}) collective-permute-start(bf16[4,256,512]{2,1,0:T(8,128)(2,1)S(1)} %get-tuple-element.8), channel_id=1, source_target_pairs={{0,4},{4,0},{8,12},{12,8},{16,20},{20,16},{24,28},{28,24},{1,5},{5... | collective-permute-start | bytes 3145736 | tf_op jit(solution)/shard_map/ppermute | solution.py:8
  39.0 24.4 %collective-permute-start.1 = (bf16[4,256,512]{2,1,0:T(8,128)(2,1)S(1)}, bf16[4,256,512]{2,1,0:T(8,128)(2,1)S(1)}, u32[]{:S(2)}, u32[]{:S(2)}) collective-permute-start(bf16[4,256,512]{2,1,0:T(8,128)(2,1)S(1)} %get-tuple-element.6), channel_id=1, source_target_pairs={{0,8},{4,12},{8,0},{12,4},{16,24},{20,28},{24,16},{28,20},{1,9},{5... | collective-permute-start | bytes 3145736 | tf_op jit(solution)/shard_map/ppermute | solution.py:8
  99.9 25.7 %collective-permute-start.2 = (f32[4,64,512]{2,1,0:T(8,128)S(1)}, f32[4,64,512]{2,1,0:T(8,128)S(1)}, u32[]{:S(2)}, u32[]{:S(2)}) collective-permute-start(f32[4,64,512]{2,1,0:T(8,128)S(1)} %get-tuple-element.10), channel_id=1, source_target_pairs={{0,16},{4,20},{8,24},{12,28},{16,0},{20,4},{24,8},{28,12},{1,17},{... | collective-permute-start | bytes 1572872 | tf_op jit(solution)/shard_map/ppermute | solution.py:8
Sparse Core Ops, SparseCore 0:
  66.2 32.3 reduce-scatter.1
where the time goes:
time: 134 us; the launch traced here: 133 us
  waiting for transfers between devices  101 us (75%)
  between operations  13.4 us (10%)
  starting transfers between devices  7.38 us (6%)
  matrix products  5.5 us (4%)
  local copies, waits for them, and re-layouts  3.47 us (3%)
  other arithmetic  2.2 us (2%)
    ppermute x3, waiting for transfers between devices, partner(): lax.ppermute(shard, axis, [(i, i ^ 1 << bit) for i in range(lax.axis_size...  68.9 us
    reduce_scatter x1, waiting for transfers between devices, local(): lax.psum_scatter(terms.astype(jnp.bfloat16), 'src', scatter_dimension=2,...  32.5 us
    ppermute x3, starting transfers between devices, partner(): lax.ppermute(shard, axis, [(i, i ^ 1 << bit) for i in range(lax.axis_size...  7.38 us
    dot_general x3, matrix products, blend(): jnp.einsum('bij,bjn->bin', weights, current, preferred_element_type=jnp.f...  5.5 us
  transfers between devices with their start and end apart: 4, of which 4 were waited for; matrix products, arithmetic and copies ran while one was open for 0% of the time, Pallas kernels for 0%

commit v1 on v0

v1 whole, which is shorter than its diff:
```python
import functools

import jax
import jax.numpy as jnp
from jax import lax
from jax.experimental import pallas as pl
from jax.experimental.pallas import tpu as pltpu
from jax.sharding import PartitionSpec as P

PARTS = 2
LAGS = (2, 4, 6)


def kernel(sizes, coef_ref, fact_ref, out_ref, *scratch):
    n_tgt, n_src, levels, blocks, half, width, parts, lags = sizes
    chunks, rows = blocks * parts, half // n_src
    fact, current, sends, part, inbox, low_send, low_recv, outbuf = scratch[:8]
    load_sem, coef_sem, lev_send, lev_recv, src_send, src_recv, low_sems, out_sem = scratch[8:]
    me = lax.axis_index("tgt")
    src = lax.axis_index("src")
    bits = n_tgt.bit_length() - 1

    def partner(level):
        step = 1 << level % bits
        return me + step * (1 - 2 * ((me // step) % 2))

    def peer(k):
        return (src + k) % n_src

    def load(level, block):
        return pltpu.make_async_copy(
            fact_ref.at[level, block], fact.at[level, block], load_sem.at[level, block]
        )

    def load_coef(c):
        return pltpu.make_async_copy(
            coef_ref.at[c // parts, :, pl.ds(pl.multiple_of((c % parts) * width, width), width)],
            current.at[0, c],
            coef_sem.at[c],
        )

    for b in range(blocks):
        load(0, b).start()
        for h in range(parts):
            load_coef(b * parts + h).start()
    for level in range(1, levels):
        for b in range(blocks):
            load(level, b).start()

    barrier = pltpu.get_barrier_semaphore()
    shifts = sorted({level % bits for level in range(levels)})
    for shift in shifts:
        pl.semaphore_signal(
            barrier, inc=1, device_id={"tgt": partner(shift)}, device_id_type=pl.DeviceIdType.MESH
        )
    for k in range(1, n_src):
        pl.semaphore_signal(
            barrier, inc=1, device_id={"src": peer(k)}, device_id_type=pl.DeviceIdType.MESH
        )

    def exchange(level, c):
        return pltpu.make_async_remote_copy(
            src_ref=sends.at[level, c],
            dst_ref=current.at[level + 1, c, pl.ds(half, half)],
            send_sem=lev_send.at[level, c],
            recv_sem=lev_recv.at[level, c],
            device_id={"tgt": partner(level)},
            device_id_type=pl.DeviceIdType.MESH,
        )

    def scatter(k, c):
        return pltpu.make_async_remote_copy(
            src_ref=part.at[c, peer(k)],
            dst_ref=inbox.at[c, k],
            send_sem=src_send.at[c, k],
            recv_sem=src_recv.at[c, k],
            device_id={"src": peer(k)},
            device_id_type=pl.DeviceIdType.MESH,
        )

    def lower(c):
        return pltpu.make_async_remote_copy(
            src_ref=low_send.at[c],
            dst_ref=low_recv.at[c],
            send_sem=low_sems.at[0, c],
            recv_sem=low_sems.at[1, c],
            device_id={"tgt": partner(levels - 1)},
            device_id_type=pl.DeviceIdType.MESH,
        )

    def write(side, c):
        columns = pl.ds(pl.multiple_of((c % parts) * width, width), width)
        return pltpu.make_async_copy(
            outbuf.at[side, c], out_ref.at[c // parts, side, :, columns], out_sem.at[side, c]
        )

    def level_stage(level, c):
        if level:
            exchange(level - 1, c).wait_recv()
        blended = jnp.dot(
            fact[level, c // parts], current[level, c], preferred_element_type=jnp.float32
        ).astype(jnp.bfloat16)
        if level < levels - 1:
            sends[level, c] = blended[half:]
            exchange(level, c).start()
            current[level + 1, c, :half] = blended[:half]
        else:
            for j in range(n_src):
                part[c, j, 0] = blended[j * rows : (j + 1) * rows]
                part[c, j, 1] = blended[half + j * rows : half + (j + 1) * rows]
            for k in range(1, n_src):
                scatter(k, c).start()

    def sum_stage(c):
        total = part[c, src].astype(jnp.float32)
        for k in range(1, n_src):
            scatter(k, c).wait_recv()
            total += inbox[c, k].astype(jnp.float32)
        low_send[c] = total[1].astype(jnp.bfloat16)
        lower(c).start()
        outbuf[0, c] = total[0]
        write(0, c).start()

    def last_stage(c):
        lower(c).wait_recv()
        outbuf[1, c] = low_recv[c].astype(jnp.float32)
        write(1, c).start()

    def first(c, carry):
        load_coef(c).wait()

        @pl.when(c % parts == 0)
        def _():
            load(0, c // parts).wait()

        level_stage(0, c)
        return carry

    pl.semaphore_wait(barrier, len(shifts) + n_src - 1)
    lax.fori_loop(0, chunks, first, 0)
    for level in range(1, levels):
        for b in range(blocks):
            load(level, b).wait()

    stages = [functools.partial(level_stage, level) for level in range(1, levels)]
    stages += [sum_stage, last_stage]

    def step(i, carry):
        for stage, lag in zip(stages, (0,) + lags):
            c = i - lag

            @pl.when(jnp.logical_and(c >= 0, c < chunks))
            def _():
                stage(c)

        return carry

    lax.fori_loop(0, chunks + lags[-1], step, 0)

    def finish(c, carry):
        for level in range(levels - 1):
            exchange(level, c).wait_send()
        for k in range(1, n_src):
            scatter(k, c).wait_send()
        lower(c).wait_send()
        write(0, c).wait()
        write(1, c).wait()
        return carry

    lax.fori_loop(0, chunks, finish, 0)


def local(n_tgt, n_src, coefficients, factors):
    levels, blocks = factors.shape[0], factors.shape[1]
    size, columns = coefficients.shape[2], coefficients.shape[3]
    half, width = size // 2, columns // PARTS
    chunks, rows = blocks * PARTS, half // n_src
    dma = pltpu.SemaphoreType.DMA
    bf16 = jnp.bfloat16
    return pl.pallas_call(
        functools.partial(
            kernel, (n_tgt, n_src, levels, blocks, half, width, PARTS, LAGS)
        ),
        out_shape=jax.ShapeDtypeStruct((blocks, 2, rows, columns), jnp.float32),
        in_specs=[pl.BlockSpec(memory_space=pl.ANY)] * 2,
        out_specs=pl.BlockSpec(memory_space=pl.ANY),
        scratch_shapes=[
            pltpu.VMEM((levels, blocks, size, size), bf16),
            pltpu.VMEM((levels, chunks, size, width), bf16),
            pltpu.VMEM((levels - 1, chunks, half, width), bf16),
            pltpu.VMEM((chunks, n_src, 2, rows, width), bf16),
            pltpu.VMEM((chunks, n_src, 2, rows, width), bf16),
            pltpu.VMEM((chunks, rows, width), bf16),
            pltpu.VMEM((chunks, rows, width), bf16),
            pltpu.VMEM((2, chunks, rows, width), jnp.float32),
            dma((levels, blocks)),
            dma((chunks,)),
            dma((levels - 1, chunks)),
            dma((levels - 1, chunks)),
            dma((chunks, n_src)),
            dma((chunks, n_src)),
            dma((2, chunks)),
            dma((2, chunks)),
        ],
        compiler_params=pltpu.CompilerParams(collective_id=0, has_side_effects=True),
    )(coefficients[:, 0], factors[:, :, 0])


def solution(mesh):
    placed = (P("tgt", "src", None, None), P(None, "tgt", "src", None, None))
    return jax.shard_map(
        functools.partial(local, mesh.shape["tgt"], mesh.shape["src"]),
        mesh=mesh,
        in_specs=placed,
        out_specs=P("tgt", None, "src", None),
        check_vma=False,
    )
```

time: 134 us -> 49.8 us (0.37)
  waiting for transfers between devices: 101 us -> 0 us
  Pallas kernels: 0 us -> 47.3 us
  between operations: 13.4 us -> 0.01 us
  starting transfers between devices: 7.38 us -> 0 us
  matrix products: 5.5 us -> 0 us
  other arithmetic: 2.2 us -> 0 us
    ppermute x3 -> x0, waiting for transfers between devices: 68.9 us -> none  [partner(): lax.ppermute(shard, axis, [(i, i ^ 1 << bit) for i in range(lax.axis_size...]
    pallas_call x0 -> x1, Pallas kernels: none -> 47.3 us  [local(): pl.pallas_call(functools.partial(kernel, (n_tgt, n_src, levels, blocks, h...]
    reduce_scatter x1 -> x0, waiting for transfers between devices: 32.5 us -> none  [local(): lax.psum_scatter(terms.astype(jnp.bfloat16), 'src', scatter_dimension=2,...]
    ppermute x3 -> x0, starting transfers between devices: 7.38 us -> none  [partner(): lax.ppermute(shard, axis, [(i, i ^ 1 << bit) for i in range(lax.axis_size...]
    dot_general x3 -> x0, matrix products: 5.5 us -> none  [blend(): jnp.einsum('bij,bjn->bin', weights, current, preferred_element_type=jnp.f...]
    convert_element_type x1 -> x0, local copies, waits for them, and re-layouts: 1.48 us -> none  [local(): terms.astype(jnp.bfloat16)]
  transfers between devices with their start and end apart: 4 -> 0, of which waited for: 4 -> 0; matrix products, arithmetic and copies ran while one was open for 0% -> 0% of each run, Pallas kernels for 0% -> 0%
where the time goes in v1:
time: 49.8 us; the launch traced here: 49.6 us
  Pallas kernels  47.3 us (95%)
  local copies, waits for them, and re-layouts  2.26 us (5%)
    pallas_call x1, Pallas kernels, local(): pl.pallas_call(functools.partial(kernel, (n_tgt, n_src, levels, blocks, h...  47.3 us
    unnamed x1, local copies, waits for them, and re-layouts  2.26 us

profile of v1, /device:TPU:0, one launch (start us, length us, event | category | flops | bytes accessed | tf_op | source)
XLA Modules:
  0.0 49.6 jit_solution(5092040162262632422)
XLA Ops:
  0.0 47.3 %shard_map.28 = f32[4,2,64,512]{3,2,1,0:T(8,128)} custom-call(bf16[4,512,512]{2,1,0:T(8,128)(2,1)} %bitcast.3, bf16[3,4,512,512]{3,2,1,0:T(8,128)(2,1)} %bitcast.2), custom_call_target="tpu_custom_call" | custom-call | tf_op jit(solution)/shard_map/pallas_call | solution.py:180
  47.4 2.3 %copy.4 = f32[4,2,64,512]{3,2,1,0:T(8,128)} copy(f32[4,2,64,512]{3,2,1,0:T(8,128)} %shard_map.28) | data formatting | bytes 2097152

commit v2 on v1

--- a/solution.py
+++ b/solution.py
@@ -7,15 +7,16 @@
 from jax.experimental.pallas import tpu as pltpu
 from jax.sharding import PartitionSpec as P
 
-PARTS = 2
-LAGS = (2, 4, 6)
+PARTS = 4
+LAGS = (3, 7, 10)
+AHEAD = 6
 
 
 def kernel(sizes, coef_ref, fact_ref, out_ref, *scratch):
-    n_tgt, n_src, levels, blocks, half, width, parts, lags = sizes
+    n_tgt, n_src, levels, blocks, half, width, parts, lags, ahead = sizes
     chunks, rows = blocks * parts, half // n_src
-    fact, current, sends, part, inbox, low_send, low_recv, outbuf = scratch[:8]
-    load_sem, coef_sem, lev_send, lev_recv, src_send, src_recv, low_sems, out_sem = scratch[8:]
+    fact, current, sends, part, inbox, low_send, low_recv = scratch[:7]
+    load_sem, coef_sem, lev_send, lev_recv, src_send, src_recv, low_sems = scratch[7:]
     me = lax.axis_index("tgt")
     src = lax.axis_index("src")
     bits = n_tgt.bit_length() - 1
@@ -88,23 +89,27 @@
             device_id_type=pl.DeviceIdType.MESH,
         )
 
-    def write(side, c):
+    def write(side, c, value):
         columns = pl.ds(pl.multiple_of((c % parts) * width, width), width)
-        return pltpu.make_async_copy(
-            outbuf.at[side, c], out_ref.at[c // parts, side, :, columns], out_sem.at[side, c]
-        )
-
-    def level_stage(level, c):
+        out_ref[c // parts, side, :, columns] = value
+
+    def level_stage(level, c, before_send=None):
         if level:
             exchange(level - 1, c).wait_recv()
-        blended = jnp.dot(
-            fact[level, c // parts], current[level, c], preferred_element_type=jnp.float32
-        ).astype(jnp.bfloat16)
+
+        def blend(rows):
+            return jnp.dot(
+                fact[level, c // parts, rows], current[level, c], preferred_element_type=jnp.float32
+            ).astype(jnp.bfloat16)
+
         if level < levels - 1:
-            sends[level, c] = blended[half:]
+            sends[level, c] = blend(pl.ds(half, half))
+            if before_send is not None:
+                before_send()
             exchange(level, c).start()
-            current[level + 1, c, :half] = blended[:half]
+            current[level + 1, c, :half] = blend(pl.ds(0, half))
         else:
+            blended = blend(pl.ds(0, 2 * half))
             for j in range(n_src):
                 part[c, j, 0] = blended[j * rows : (j + 1) * rows]
                 part[c, j, 1] = blended[half + j * rows : half + (j + 1) * rows]
@@ -118,35 +123,42 @@
             total += inbox[c, k].astype(jnp.float32)
         low_send[c] = total[1].astype(jnp.bfloat16)
         lower(c).start()
-        outbuf[0, c] = total[0]
-        write(0, c).start()
+        write(0, c, total[0])
 
     def last_stage(c):
         lower(c).wait_recv()
-        outbuf[1, c] = low_recv[c].astype(jnp.float32)
-        write(1, c).start()
-
-    def first(c, carry):
+        write(1, c, low_recv[c].astype(jnp.float32))
+
+    def first(c, before_send=None):
         load_coef(c).wait()
 
         @pl.when(c % parts == 0)
         def _():
             load(0, c // parts).wait()
 
-        level_stage(0, c)
+        level_stage(0, c, before_send)
+
+    def later(level, c):
+        @pl.when(c % parts == 0)
+        def _():
+            load(level, c // parts).wait()
+
+        level_stage(level, c)
+
+    def looped(c, carry):
+        first(c)
         return carry
 
-    pl.semaphore_wait(barrier, len(shifts) + n_src - 1)
-    lax.fori_loop(0, chunks, first, 0)
-    for level in range(1, levels):
-        for b in range(blocks):
-            load(level, b).wait()
-
-    stages = [functools.partial(level_stage, level) for level in range(1, levels)]
+    first(jnp.int32(0), lambda: pl.semaphore_wait(barrier, len(shifts) + n_src - 1))
+    lax.fori_loop(1, ahead, looped, 0)
+
+    stages = [functools.partial(later, level) for level in range(1, levels)]
     stages += [sum_stage, last_stage]
+    if ahead < chunks:
+        stages.append(first)
 
     def step(i, carry):
-        for stage, lag in zip(stages, (0,) + lags):
+        for stage, lag in zip(stages, (0,) + lags + (-ahead,)):
             c = i - lag
 
             @pl.when(jnp.logical_and(c >= 0, c < chunks))
@@ -163,8 +175,6 @@
         for k in range(1, n_src):
             scatter(k, c).wait_send()
         lower(c).wait_send()
-        write(0, c).wait()
-        write(1, c).wait()
         return carry
 
     lax.fori_loop(0, chunks, finish, 0)
@@ -179,11 +189,11 @@
     bf16 = jnp.bfloat16
     return pl.pallas_call(
         functools.partial(
-            kernel, (n_tgt, n_src, levels, blocks, half, width, PARTS, LAGS)
+            kernel, (n_tgt, n_src, levels, blocks, half, width, PARTS, LAGS, min(AHEAD, chunks))
         ),
-        out_shape=jax.ShapeDtypeStruct((blocks, 2, rows, columns), jnp.float32),
+        out_shape=pltpu.VMEM((blocks, 2, rows, columns), jnp.float32),
         in_specs=[pl.BlockSpec(memory_space=pl.ANY)] * 2,
-        out_specs=pl.BlockSpec(memory_space=pl.ANY),
+        out_specs=pl.BlockSpec(memory_space=pltpu.VMEM),
         scratch_shapes=[
             pltpu.VMEM((levels, blocks, size, size), bf16),
             pltpu.VMEM((levels, chunks, size, width), bf16),
@@ -192,14 +202,12 @@
             pltpu.VMEM((chunks, n_src, 2, rows, width), bf16),
             pltpu.VMEM((chunks, rows, width), bf16),
             pltpu.VMEM((chunks, rows, width), bf16),
-            pltpu.VMEM((2, chunks, rows, width), jnp.float32),
             dma((levels, blocks)),
             dma((chunks,)),
             dma((levels - 1, chunks)),
             dma((levels - 1, chunks)),
             dma((chunks, n_src)),
             dma((chunks, n_src)),
-            dma((2, chunks)),
             dma((2, chunks)),
         ],
         compiler_params=pltpu.CompilerParams(collective_id=0, has_side_effects=True),

time: 49.8 us -> 46.8 us (0.940)
  Pallas kernels: 47.3 us -> 45.6 us
  local copies, waits for them, and re-layouts: 2.26 us -> 0.97 us
    pallas_call x1, Pallas kernels: 47.3 us -> 45.6 us  [local(): pl.pallas_call(functools.partial(kernel, (n_tgt, n_src, levels, blocks, h...]
    unnamed x1, local copies, waits for them, and re-layouts: 2.26 us -> 0.97 us
where the time goes in v2:
time: 46.8 us; the launch traced here: 46.6 us
  Pallas kernels  45.6 us (97%)
  local copies, waits for them, and re-layouts  0.97 us (2%)
    pallas_call x1, Pallas kernels, local(): pl.pallas_call(functools.partial(kernel, (n_tgt, n_src, levels, blocks, h...  45.6 us
    unnamed x1, local copies, waits for them, and re-layouts  0.97 us

profile of v2, /device:TPU:0, one launch (start us, length us, event | category | flops | bytes accessed | tf_op | source)
XLA Modules:
  0.0 46.6 jit_solution(5144252803197296064)
XLA Ops:
  0.0 45.6 %shard_map.28 = f32[4,2,64,512]{3,2,1,0:T(8,128)S(1)} custom-call(bf16[4,512,512]{2,1,0:T(8,128)(2,1)} %bitcast.3, bf16[3,4,512,512]{3,2,1,0:T(8,128)(2,1)} %bitcast.2), custom_call_target="tpu_custom_call" | custom-call | tf_op jit(solution)/shard_map/pallas_call | solution.py:190
  45.6 1.0 %copy.4 = f32[4,2,64,512]{3,2,1,0:T(8,128)} copy(f32[4,2,64,512]{3,2,1,0:T(8,128)S(1)} %shard_map.28) | data formatting | bytes 2097152
